TPU v7x, 32 devices: a whole 2x2x4 slice. The times are simulated.
32 devices in a mesh: row: 4 (over y, x), col: 8 (over z, core).
Axes of the slice: x: 2, y: 2, z: 4, core: 2. Of those that a mesh axis runs over, the one named last changes fastest.
Arguments:
- stiffness: float32 [12, 4, 128, 6144], P(None, 'row', None, 'col'), may hold values from -8 to 8
- lower_first: float32 [1024, 10, 4, 128], P('col', None, 'row'), may hold values from -0.1875 to 0.1875
- lower_second: float32 [1024, 8, 4, 128], P('col', None, 'row'), may hold values from -0.1875 to 0.1875
- diag_inv: float32 [2, 1024, 2, 4, 128], P(None, 'col', None, 'row'), as said below
Outputs:
- reduced: float32 [12, 4, 128, 6144], P(None, 'row', None, 'col')
Inputs may be any that keep to these rules, and one draw needn't show every extreme that they name: Each block of diag_inv, read as a 1024 x 1024 matrix, is zero above its diagonal and has a positive diagonal.
All inputs are finite; a program needn't handle non-finite values.
Results may differ from a plain program's by a relative error of at most 0.000086.
Values sent between devices are 32-bit elements; how exact they have to be, the bound alone decides.
A program may use at most 128 MiB of HBM per device.

v0:
```python
import jax
import jax.numpy as jnp
from jax import lax
from jax.sharding import PartitionSpec as P


def product(left, right):
    return jnp.dot(left, right, precision=lax.Precision.HIGH, preferred_element_type=jnp.float32)


def apply_cols(columns, factor):
    return lax.dot_general(
        columns,
        factor,
        (((0,), (0,)), ((), ())),
        precision=lax.Precision.HIGH,
        preferred_element_type=jnp.float32,
    )


def shards(stiffness, lower_first, lower_second, diag_inv):
    cycles = stiffness.shape[0]
    rblk = stiffness.shape[2]
    cdev = stiffness.shape[3]
    pcount = diag_inv.shape[2]
    nrow = lax.axis_size("row")
    nb = diag_inv.shape[1] * lax.axis_size("col")
    height = pcount * rblk
    matrix_rows = stiffness.reshape(cycles * rblk, cdev)
    inv_cols = lax.all_gather(diag_inv, "col", axis=1, tiled=True)
    inverse = inv_cols.reshape(2, nb, height)

    def own_rows(solved):
        grouped = solved.reshape(pcount, nrow, rblk, cdev)
        mine = lax.dynamic_slice_in_dim(grouped, lax.axis_index("row"), 1, 1)
        return mine.reshape(height, cdev)

    w_first = lax.psum(product(inverse[0], matrix_rows[:height]), "row")
    coupling = lax.all_gather(lower_first[:, :pcount], "col", axis=0, tiled=True).reshape(
        nb, height
    )
    w_second = lax.psum(
        product(inverse[1], matrix_rows[height : 2 * height] - apply_cols(coupling, w_first)), "row"
    )
    pieces = (
        lax.all_gather(lower_first[:, pcount:], "col", axis=0, tiled=True),
        lax.all_gather(lower_second, "col", axis=0, tiled=True),
    )
    count = pieces[0].shape[0]
    first_piece = pieces[0].reshape(count, -1)
    second_piece = pieces[1].reshape(count, -1)
    remain = (
        matrix_rows[2 * height :]
        - apply_cols(first_piece, w_first)
        - apply_cols(second_piece, w_second)
    )
    stacked = jnp.concatenate([own_rows(w_first), own_rows(w_second), remain], axis=0)
    return stacked.reshape(cycles, 1, rblk, cdev)


def solution(mesh):
    placed = (
        P(None, "row", None, "col"),
        P("col", None, "row", None),
        P("col", None, "row", None),
        P(None, "col", None, "row", None),
    )
    return jax.shard_map(
        shards, mesh=mesh, in_specs=placed, out_specs=P(None, "row", None, "col"), check_vma=False
    )
```

profile of v0, /device:TPU:0, one launch (start us, length us, event | category | flops | bytes accessed | tf_op | source)
XLA Modules:
  0.0 369.2 jit_solution(9611690720741950493)
XLA Ops:
  6.5 0.7 all-gather.5.cloned.1.call-update
  7.3 0.0 all-gather.7.cloned.1.call-start
  7.3 1.6 slice.37
  8.9 0.0 all-reduce.3.cloned.1.call-start
  8.9 1.5 fusion.16
  10.4 30.4 %all-gather.5.cloned.1.call-done = f32[2,1024,2,1,128]{4,3,2,1,0:T(1,128)} async-done(((f32[2,128,2,1,128]{4,3,2,1,0:T(1,128)}), f32[2,1024,2,1,128]{4,3,2,1,0:T(1,128)}) %all-gather.5.cloned.1.call-update) | async-done | bytes 2097168 | tf_op jit(solution)/shard_map/all_gather | solution.py:30
  40.8 7.8 %slice_reduce_fusion = (f32[1024,2,128]{2,1,0:T(2,128)S(1)}, f32[1024,2,128]{2,1,0:T(2,128)S(1)}) fusion(f32[2,1024,2,1,128]{4,3,2,1,0:T(1,128)} %all-gather.5.cloned.1.call-done), kind=kLoop, calls=%fused_computation.19 | loop fusion | bytes 4194304 | tf_op jit(solution)/shard_map/slice | solution.py:43
  48.7 3.1 fusion.13
  51.8 0.0 all-reduce.5.cloned.1.call-start
  51.9 0.3 copy.21
  52.2 12.0 %all-gather.7.cloned.1.call-done = f32[1024,2,1,128]{3,1,2,0:T(2,128)} async-done(((f32[128,2,1,128]{3,1,2,0:T(2,128)}), f32[1024,2,1,128]{3,1,2,0:T(2,128)}) %all-gather.7.cloned.1.call-update) | async-done | bytes 1048592 | tf_op jit(solution)/shard_map/all_gather | solution.py:39
  64.1 89.7 %all-reduce.3.cloned.1.call-done = f32[1024,768]{1,0:T(8,128)} async-done(((f32[1024,768]{1,0:T(8,128)}), f32[1024,768]{1,0:T(8,128)}) %all-reduce.3.cloned.1.call-update) | async-done | bytes 3145744 | tf_op jit(solution)/shard_map/psum | solution.py:38
  153.8 4.8 %fusion.8 = f32[256,768]{0,1:T(8,128)S(1)} fusion(f32[256,768]{0,1:T(8,128)S(1)} %copy.21, f32[1024,768]{1,0:T(8,128)} %all-reduce.3.cloned.1.call-done, f32[128,8,2,128]{3,2,1,0:T(2,128)} %bitcast.76), kind=kOutput, calls=%fused_computation.11 | convolution fusion | flops 1208156160 | bytes 5767168 | tf_op jit(solution)/shard_map/dot_general | solution.py:12
  158.6 3.1 convolution_bitcast_fusion
  161.7 0.0 all-gather.11.cloned.1.call-start
  161.8 0.5 all-gather.11.cloned.1.call-update
  162.3 0.2 all-gather.9.cloned.1.call-start
  162.6 0.8 slice.41
  163.4 3.8 %slice.39 = f32[8,1,128,768]{3,2,1,0:T(8,128)} slice(f32[12,1,128,768]{3,2,1,0:T(8,128)} %param.4), slice={[4:12], [0:1], [0:128], [0:768]} | slice | bytes 6291456 | tf_op jit(solution)/shard_map/slice | solution.py:53
  167.2 4.1 %copy.22 = f32[1024,768]{0,1:T(8,128)} copy(f32[1024,768]{1,0:T(8,128)} %bitcast.65) | data formatting | bytes 6291456 | tf_op jit(solution)/shard_map/slice | solution.py:53
  171.3 0.9 constant_dynamic-slice_fusion
  172.3 2.3 copy.20
  174.6 74.3 %all-reduce.5.cloned.1.call-done = f32[1024,768]{0,1:T(8,128)} async-done(((f32[1024,768]{0,1:T(8,128)}), f32[1024,768]{0,1:T(8,128)}) %all-reduce.5.cloned.1.call-update) | async-done | bytes 3145744 | tf_op jit(solution)/shard_map/psum | solution.py:42
  248.8 5.1 %reshape.36 = f32[2,4,128,768]{2,1,0,3:T(4,128)} reshape(f32[1024,768]{0,1:T(8,128)} %all-reduce.5.cloned.1.call-done) | data formatting | bytes 6291456 | tf_op jit(solution)/shard_map/reshape | solution.py:34
  254.0 4.6 %dynamic-slice_reduce_fusion = f32[2,128,768]{1,0,2:T(2,128)S(1)} fusion(f32[2,4,128,768]{2,1,0,3:T(4,128)} %reshape.36, s32[]{:T(128)S(6)} %select_n.4), kind=kLoop, calls=%fused_computation.22 | loop fusion | bytes 1572868 | tf_op jit(solution)/shard_map/dynamic_slice | solution.py:35
  258.5 0.9 copy.54
  259.5 37.7 %all-gather.11.cloned.1.call-done = f32[1024,8,1,128]{3,1,2,0:T(8,128)} async-done(((f32[128,8,1,128]{3,1,2,0:T(8,128)}), f32[1024,8,1,128]{3,1,2,0:T(8,128)}) %all-gather.11.cloned.1.call-update) | async-done | bytes 4194320 | tf_op jit(solution)/shard_map/all_gather | solution.py:47
  297.2 9.6 %fusion = f32[768,1024]{1,0:T(8,128)} fusion(f32[1024,768]{0,1:T(8,128)} %all-reduce.5.cloned.1.call-done, f32[128,8,8,128]{3,2,1,0:T(8,128)} %bitcast.66), kind=kOutput, calls=%fused_computation.1 | convolution fusion | flops 4831838208 | bytes 10485760 | tf_op jit(solution)/shard_map/dot_general | solution.py:12
  306.8 37.6 %all-gather.9.cloned.1.call-done = f32[1024,8,1,128]{3,1,2,0:T(8,128)} async-done(((f32[128,8,1,128]{3,1,2,0:T(8,128)}), f32[1024,8,1,128]{3,1,2,0:T(8,128)}) %all-gather.9.cloned.1.call-update) | async-done | bytes 4194320 | tf_op jit(solution)/shard_map/all_gather | solution.py:46
  344.3 9.4 %bitcast_subtract_fusion = f32[1024,768]{0,1:T(8,128)S(1)} fusion(f32[768,1024]{1,0:T(8,128)} %fusion, f32[1024,768]{0,1:T(8,128)} %copy.22, f32[1024,768]{1,0:T(8,128)S(1)} %copy-done, f32[128,8,8,128]{3,2,1,0:T(8,128)} %bitcast.69), kind=kOutput, calls=%fused_computation.7 | convolution fusion | flops 4833411072 | bytes 16777216 | tf_op jit(solution)/shard_map/dot_general | solution.py:12
  353.8 2.6 pad_maximum_fusion
  356.4 6.0 %copy.18 = f32[1536,768]{1,0:T(8,128)} copy(f32[1536,768]{0,1:T(8,128)} %pad_maximum_fusion) | data formatting | bytes 9437184 | tf_op jit(solution)/shard_map/concatenate | solution.py:57
  (13 shorter events, 0.1 us)
Async XLA Ops:
  6.5 34.3 %all-gather.5.cloned.1.call-start = ((), (), s32[]{:S(2)}) async-start(), calls=%async_computation | async-start | bytes 2359296 | tf_op jit(solution)/shard_map/all_gather | solution.py:30
  7.3 56.9 %all-gather.7.cloned.1.call-start = ((), (), s32[]{:S(2)}) async-start(), calls=%async_computation.2 | async-start | bytes 1179648 | tf_op jit(solution)/shard_map/all_gather | solution.py:39
  8.9 144.9 %all-reduce.3.cloned.1.call-start = ((), (), s32[]{:S(2)}) async-start(), calls=%async_computation.1 | async-start | bytes 6291456 | tf_op jit(solution)/shard_map/psum | solution.py:38
  51.8 197.0 %all-reduce.5.cloned.1.call-start = ((), (), s32[]{:S(2)}) async-start(), calls=%async_computation.3 | async-start | bytes 6291456 | tf_op jit(solution)/shard_map/psum | solution.py:42
  158.6 4.0 %copy-start.3 = (f32[128,10,1,128]{3,2,1,0:T(1,128)S(1)}, f32[128,10,1,128]{3,2,1,0:T(1,128)}, u32[]{:S(2)}) copy-start(f32[128,10,1,128]{3,2,1,0:T(1,128)} %param.5) | copy-start | bytes 1966084
  161.7 135.4 %all-gather.11.cloned.1.call-start = ((), (), s32[]{:S(2)}) async-start(), calls=%async_computation.5 | async-start | bytes 4718592 | tf_op jit(solution)/shard_map/all_gather | solution.py:47
  162.3 182.0 %all-gather.9.cloned.1.call-start = ((), (), s32[]{:S(2)}) async-start(), calls=%async_computation.4 | async-start | bytes 4718592 | tf_op jit(solution)/shard_map/all_gather | solution.py:46
  167.2 4.1 %copy-start = (f32[1024,768]{1,0:T(8,128)S(1)}, f32[1024,768]{1,0:T(8,128)}, u32[]{:S(2)}) copy-start(f32[1024,768]{1,0:T(8,128)} %all-reduce.3.cloned.1.call-done) | copy-start | bytes 9437188
  344.3 9.4 %copy-start.1 = (f32[256,768]{0,1:T(8,128)S(1)}, f32[256,768]{0,1:T(8,128)}, u32[]{:S(2)}) copy-start(f32[256,768]{0,1:T(8,128)} %copy.20) | copy-start | bytes 2359300
  344.3 9.4 %copy-start.2 = (f32[96,8,2,128]{3,1,2,0:T(8,128)S(1)}, f32[96,8,2,128]{3,1,2,0:T(8,128)}, u32[]{:S(2)}) copy-start(f32[96,8,2,128]{3,1,2,0:T(8,128)} %copy.54) | copy-start | bytes 2359300
Sparse Core Ops, SparseCore 0:
  8.9 31.8 all-gather.4
  42.4 21.6 all-gather.6
  67.2 86.5 all-reduce.2
  161.9 86.9 all-reduce.4
  250.3 46.8 all-gather.10
  298.6 45.6 all-gather.8
where the time goes:
time: 370 us; the launch traced here: 369 us
  waiting for transfers between devices  283 us (76%)
  local copies, waits for them, and re-layouts  39.8 us (11%)
  matrix products  30 us (8%)
  between operations  13.6 us (4%)
    psum x1, waiting for transfers between devices, shards(): w_first = lax.psum(product(inverse[0], matrix_rows[:height]), 'row')  89.7 us
    psum x1, waiting for transfers between devices, shards(): lax.psum(product(inverse[1], matrix_rows[height:2 * height] - apply_cols(...  74.3 us
    all_gather x1, waiting for transfers between devices, shards(): lax.all_gather(lower_second, 'col', axis=0, tiled=True)  37.7 us
    all_gather x1, waiting for transfers between devices, shards(): lax.all_gather(lower_first[:, pcount:], 'col', axis=0, tiled=True)  37.6 us
    all_gather x1, waiting for transfers between devices, shards(): inv_cols = lax.all_gather(diag_inv, 'col', axis=1, tiled=True)  30.4 us
    dot_general x3, matrix products, apply_cols(): lax.dot_general(columns, factor, (((0,), (0,)), ((), ())), precision=lax....  23.8 us
    all_gather x1, waiting for transfers between devices, shards(): lax.all_gather(lower_first[:, :pcount], 'col', axis=0, tiled=True)  12 us
    slice x2, local copies, waits for them, and re-layouts, shards(): matrix_rows[2 * height:] - apply_cols(first_piece, w_first)  7.89 us
  transfers between devices with their start and end apart: 6, of which 6 were waited for; matrix products, arithmetic and copies ran while one was open for 13% of the time, Pallas kernels for 0%

commit v1 on v0

--- a/solution.py
+++ b/solution.py
@@ -39,9 +39,9 @@
     coupling = lax.all_gather(lower_first[:, :pcount], "col", axis=0, tiled=True).reshape(
         nb, height
     )
-    w_second = lax.psum(
-        product(inverse[1], matrix_rows[height : 2 * height] - apply_cols(coupling, w_first)), "row"
-    )
+    body = product(inverse[1], matrix_rows[height : 2 * height] - apply_cols(coupling, w_first))
+    s_next = lax.all_gather(body, axis_name="row")
+    w_second = jnp.sum(s_next, 0)
     pieces = (
         lax.all_gather(lower_first[:, pcount:], "col", axis=0, tiled=True),
         lax.all_gather(lower_second, "col", axis=0, tiled=True),

time: 370 us -> 406 us (1.097)
  waiting for transfers between devices: 283 us -> 301 us
  other arithmetic: 2.59 us -> 12.5 us
  local copies, waits for them, and re-layouts: 39.8 us -> 47.3 us
    all_gather x0 -> x1, waiting for transfers between devices: none -> 114 us  [shards(): s_next = lax.all_gather(body, axis_name='row')]
    psum x1 -> x0, waiting for transfers between devices: 74.3 us -> none  [shards(): lax.psum(product(inverse[1], matrix_rows[height:2 * height] - apply_cols(...]
    all_gather x1, waiting for transfers between devices: 37.7 us -> 15.9 us  [shards(): lax.all_gather(lower_second, 'col', axis=0, tiled=True)]
    all_gather x0 -> x1, local copies, waits for them, and re-layouts: none -> 15.7 us  [shards(): s_next = lax.all_gather(body, axis_name='row')]
    reduce_sum x0 -> x1, other arithmetic: none -> 9.95 us  [shards(): w_second = jnp.sum(s_next, 0)]
    reshape x1 -> x0, local copies, waits for them, and re-layouts: 5.13 us -> none  [own_rows(): grouped = solved.reshape(pcount, nrow, rblk, cdev)]
  transfers between devices with their start and end apart: 6 -> 6, of which waited for: 6 -> 6; matrix products, arithmetic and copies ran while one was open for 13% -> 15% of each run, Pallas kernels for 0% -> 0%
where the time goes in v1:
time: 406 us
  waiting for transfers between devices  301 us (74%)
  local copies, waits for them, and re-layouts  47.3 us (12%)
  matrix products  30.4 us (7%)
  between operations  13.6 us (3%)
  other arithmetic  12.5 us (3%)
    all_gather x1, waiting for transfers between devices, shards(): s_next = lax.all_gather(body, axis_name='row')  114 us
    psum x1, waiting for transfers between devices, shards(): w_first = lax.psum(product(inverse[0], matrix_rows[:height]), 'row')  89.7 us
    all_gather x1, waiting for transfers between devices, shards(): lax.all_gather(lower_first[:, pcount:], 'col', axis=0, tiled=True)  38.1 us
    all_gather x1, waiting for transfers between devices, shards(): inv_cols = lax.all_gather(diag_inv, 'col', axis=1, tiled=True)  30.4 us
    dot_general x3, matrix products, apply_cols(): lax.dot_general(columns, factor, (((0,), (0,)), ((), ())), precision=lax....  24.1 us
    all_gather x1, waiting for transfers between devices, shards(): lax.all_gather(lower_second, 'col', axis=0, tiled=True)  15.9 us
    all_gather x1, local copies, waits for them, and re-layouts, shards(): s_next = lax.all_gather(body, axis_name='row')  15.7 us
    all_gather x1, waiting for transfers between devices, shards(): lax.all_gather(lower_first[:, :pcount], 'col', axis=0, tiled=True)  12 us
  transfers between devices with their start and end apart: 6, of which 6 were waited for; matrix products, arithmetic and copies ran while one was open for 15% of the time, Pallas kernels for 0%

profile of v1, /device:TPU:0, one launch (start us, length us, event | category | flops | bytes accessed | tf_op | source)
XLA Modules:
  0.0 405.6 jit_solution(12816044676412542944)
XLA Ops:
  6.5 0.7 all-gather.7.cloned.1.call-update
  7.3 1.6 slice.37
  8.9 0.0 all-reduce.2.cloned.1.call-start
  8.9 1.5 fusion.16
  10.4 30.4 %all-gather.7.cloned.1.call-done = f32[2,1024,2,1,128]{4,3,2,1,0:T(1,128)} async-done(((f32[2,128,2,1,128]{4,3,2,1,0:T(1,128)}), f32[2,1024,2,1,128]{4,3,2,1,0:T(1,128)}) %all-gather.7.cloned.1.call-update) | async-done | bytes 2097168 | tf_op jit(solution)/shard_map/all_gather | solution.py:30
  40.8 7.8 %slice_reduce_fusion = (f32[1024,2,128]{2,1,0:T(2,128)S(1)}, f32[1024,2,128]{2,1,0:T(2,128)S(1)}) fusion(f32[2,1024,2,1,128]{4,3,2,1,0:T(1,128)} %all-gather.7.cloned.1.call-done), kind=kLoop, calls=%fused_computation.19 | loop fusion | bytes 4194304 | tf_op jit(solution)/shard_map/slice | solution.py:42
  48.7 3.1 fusion.13
  51.8 0.0 all-gather.15.cloned.1.call-start
  51.9 0.3 copy.24
  52.2 12.0 %all-gather.9.cloned.1.call-done = f32[1024,2,1,128]{3,1,2,0:T(2,128)} async-done(((f32[128,2,1,128]{3,1,2,0:T(2,128)}), f32[1024,2,1,128]{3,1,2,0:T(2,128)}) %all-gather.9.cloned.1.call-update) | async-done | bytes 1048592 | tf_op jit(solution)/shard_map/all_gather | solution.py:39
  64.1 89.7 %all-reduce.2.cloned.1.call-done = f32[1024,768]{1,0:T(8,128)} async-done(((f32[1024,768]{1,0:T(8,128)}), f32[1024,768]{1,0:T(8,128)}) %all-reduce.2.cloned.1.call-update) | async-done | bytes 3145744 | tf_op jit(solution)/shard_map/psum | solution.py:38
  153.8 4.8 %fusion.8 = f32[256,768]{0,1:T(8,128)S(1)} fusion(f32[256,768]{0,1:T(8,128)S(1)} %copy.24, f32[1024,768]{1,0:T(8,128)} %all-reduce.2.cloned.1.call-done, f32[128,8,2,128]{3,2,1,0:T(2,128)} %bitcast.72), kind=kOutput, calls=%fused_computation.11 | convolution fusion | flops 1208156160 | bytes 5767168 | tf_op jit(solution)/shard_map/dot_general | solution.py:12
  158.6 3.1 convolution_bitcast_fusion
  161.8 0.5 all-gather.13.cloned.1.call-update
  162.3 0.2 all-gather.11.cloned.1.call-start
  162.6 0.8 slice.41
  163.4 1.9 slice-done
  165.3 2.3 copy.26
  167.6 1.3 constant_dynamic-slice_fusion.1
  169.0 1.2 copy.23
  170.2 114.1 %all-gather.15.cloned.1.call-done = f32[4096,768]{0,1:T(8,128)} async-done(((f32[1024,768]{0,1:T(8,128)}), f32[4096,768]{0,1:T(8,128)}) %all-gather.15.cloned.1.call-update) | async-done | bytes 12582928 | tf_op jit(solution)/shard_map/all_gather | solution.py:43
  284.3 15.7 %reshape.41 = f32[4,1024,768]{1,0,2:T(4,128)} reshape(f32[4096,768]{0,1:T(8,128)} %all-gather.15.cloned.1.call-done) | data formatting | bytes 25165824 | tf_op jit(solution)/shard_map/all_gather | solution.py:43
  300.0 9.9 %reduce_sum.9 = f32[1024,768]{0,1:T(8,128)S(1)} reduce(f32[4,1024,768]{1,0,2:T(4,128)} %reshape.41, f32[]{:T(128)} %constant.10.clone.1), dimensions={0}, to_apply=%region_1.0 | reduce | flops 2359296 | bytes 15728644 | tf_op jit(solution)/shard_map/reduce_sum | solution.py:44
  309.9 2.4 copy.16
  312.3 2.1 constant_dynamic-slice_fusion
  314.4 2.3 copy.25
  316.7 15.9 %all-gather.13.cloned.1.call-done = f32[1024,8,1,128]{3,1,2,0:T(8,128)} async-done(((f32[128,8,1,128]{3,1,2,0:T(8,128)}), f32[1024,8,1,128]{3,1,2,0:T(8,128)}) %all-gather.13.cloned.1.call-update) | async-done | bytes 4194320 | tf_op jit(solution)/shard_map/all_gather | solution.py:47
  332.6 9.1 %fusion = f32[768,1024]{1,0:T(8,128)} fusion(f32[1024,768]{0,1:T(8,128)S(1)} %reduce_sum.9, f32[128,8,8,128]{3,2,1,0:T(8,128)} %bitcast.63), kind=kOutput, calls=%fused_computation.1 | convolution fusion | flops 4831838208 | bytes 10485760 | tf_op jit(solution)/shard_map/dot_general | solution.py:12
  341.7 38.1 %all-gather.11.cloned.1.call-done = f32[1024,8,1,128]{3,1,2,0:T(8,128)} async-done(((f32[128,8,1,128]{3,1,2,0:T(8,128)}), f32[1024,8,1,128]{3,1,2,0:T(8,128)}) %all-gather.11.cloned.1.call-update) | async-done | bytes 4194320 | tf_op jit(solution)/shard_map/all_gather | solution.py:46
  379.8 10.3 %bitcast_subtract_fusion = f32[1024,768]{0,1:T(8,128)S(1)} fusion(f32[768,1024]{1,0:T(8,128)} %fusion, f32[1024,768]{0,1:T(8,128)} %copy.26, f32[1024,768]{1,0:T(8,128)} %all-reduce.2.cloned.1.call-done, f32[128,8,8,128]{3,2,1,0:T(8,128)} %bitcast.66), kind=kOutput, calls=%fused_computation.7 | convolution fusion | flops 4833411072 | bytes 16777216 | tf_op jit(solution)/shard_map/dot_general | solution.py:12
  390.1 2.6 pad_maximum_fusion
  392.7 6.0 %copy.21 = f32[1536,768]{1,0:T(8,128)} copy(f32[1536,768]{0,1:T(8,128)} %pad_maximum_fusion) | data formatting | bytes 9437184 | tf_op jit(solution)/shard_map/concatenate | solution.py:57
  (14 shorter events, 0.2 us)
Async XLA Ops:
  6.5 34.3 %all-gather.7.cloned.1.call-start = ((), (), s32[]{:S(2)}) async-start(), calls=%async_computation | async-start | bytes 2359296 | tf_op jit(solution)/shard_map/all_gather | solution.py:30
  7.3 56.9 %all-gather.9.cloned.1.call-start = ((), (), s32[]{:S(2)}) async-start(), calls=%async_computation.2 | async-start | bytes 1179648 | tf_op jit(solution)/shard_map/all_gather | solution.py:39
  8.9 144.9 %all-reduce.2.cloned.1.call-start = ((), (), s32[]{:S(2)}) async-start(), calls=%async_computation.1 | async-start | bytes 6291456 | tf_op jit(solution)/shard_map/psum | solution.py:38
  51.8 232.4 %all-gather.15.cloned.1.call-start = ((), (), s32[]{:S(2)}) async-start(), calls=%async_computation.5 | async-start | bytes 15728640 | tf_op jit(solution)/shard_map/all_gather | solution.py:43
  158.6 4.0 copy-start.2
  161.7 170.9 %all-gather.13.cloned.1.call-start = ((), (), s32[]{:S(2)}) async-start(), calls=%async_computation.4 | async-start | bytes 4718592 | tf_op jit(solution)/shard_map/all_gather | solution.py:47
  162.3 217.5 %all-gather.11.cloned.1.call-start = ((), (), s32[]{:S(2)}) async-start(), calls=%async_computation.3 | async-start | bytes 4718592 | tf_op jit(solution)/shard_map/all_gather | solution.py:46
  163.4 1.9 slice-start
  379.8 10.3 %copy-start = (f32[256,768]{0,1:T(8,128)S(1)}, f32[256,768]{0,1:T(8,128)}, u32[]{:S(2)}) copy-start(f32[256,768]{0,1:T(8,128)} %copy.23) | copy-start | bytes 2359300
  379.8 10.3 %copy-start.1 = (f32[256,768]{0,1:T(8,128)S(1)}, f32[256,768]{0,1:T(8,128)}, u32[]{:S(2)}) copy-start(f32[256,768]{0,1:T(8,128)} %copy.25) | copy-start | bytes 2359300
Sparse Core Ops, SparseCore 0:
  8.9 31.8 all-gather.6
  42.4 21.6 all-gather.8
  67.2 86.5 all-reduce.1
  161.9 122.3 all-gather.14
  285.7 46.8 all-gather.12
  334.1 45.6 all-gather.10
